TPU v7x, 256 devices: a whole 4x4x8 slice. The times are simulated.
256 devices in a mesh: wide: 64 (over y, z, core), narrow: 4 (over x).
Axes of the slice: x: 4, y: 4, z: 8, core: 2. Of those that a mesh axis runs over, the one named last changes fastest.
Arguments:
- residual_in: bfloat16 [128, 7168], P('wide', 'narrow'), may hold values from -2 to 2
- query_nope: bfloat16 [128, 64, 128], P('wide', 'narrow'), may hold values from -6 to 6
- query_rope: bfloat16 [128, 64, 64], P('wide', 'narrow'), may hold values from -8 to 8
- absorb_key: bfloat16 [64, 128, 512], P('narrow'), may hold values from -0.5 to 0.5
- absorb_value: bfloat16 [64, 512, 128], P('narrow'), may hold values from -0.25 to 0.25
- latent_cache: bfloat16 [128, 2048, 576], P('wide'), may hold values from -8 to 8
- cache_lengths: int32 [128], P('wide'), may hold values from 256 to 2048, as said below
- slot_rows: int32 [128], replicated, may hold values from 0 to 127, each once
- out_proj: bfloat16 [8192, 7168], P('wide', 'narrow'), may hold values from -0.0625 to 0.0625
- norm_gain: bfloat16 [7168], P('narrow'), may hold values from 0.25 to 1.75
- gate_weight: bfloat16 [7168, 18432], P('narrow', 'wide'), may hold values from -0.0625 to 0.0625
- up_weight: bfloat16 [7168, 18432], P('narrow', 'wide'), may hold values from -0.0625 to 0.0625
- down_weight: bfloat16 [18432, 7168], P('wide', 'narrow'), may hold values from -0.046875 to 0.046875
Outputs:
- residual_out: bfloat16 [128, 7168], P('wide', 'narrow')
Inputs may be any that keep to these rules, and one draw needn't show every extreme that they name: `cache_lengths`: every slot has at least 256 live positions; in every draw some slot is full. `slot_rows`: each batch row is named by exactly one slot.
All inputs are finite; a program needn't handle non-finite values.
Results may differ from a plain program's by a relative error of at most 0.009.
Values may be sent and summed in bfloat16 or wider, within the bound.
A program may use at most 64 MiB of HBM per device.

v0:
```python
import math
import jax
import jax.numpy as jnp
from jax import lax
from jax.sharding import PartitionSpec as P

D = 7168


def shards(
    residual_in,
    query_nope,
    query_rope,
    absorb_key,
    absorb_value,
    latent_cache,
    cache_lengths,
    slot_rows,
    out_proj,
    norm_gain,
    gate_weight,
    up_weight,
    down_weight,
):
    slot_count = latent_cache.shape[0]
    head_size = query_nope.shape[2]
    latent_width = absorb_key.shape[2]
    group_index = lax.axis_index("wide")
    packed_queries = jnp.concatenate([query_nope, query_rope], axis=2)
    gathered = lax.all_gather(packed_queries, "wide", axis=0, tiled=True)
    my_rows = lax.dynamic_slice_in_dim(slot_rows, group_index * slot_count, slot_count)
    selected = jnp.take(gathered, my_rows, axis=0)
    query_latent = jnp.einsum(
        "rhd,hdc->rhc", selected[:, :, :head_size], absorb_key, preferred_element_type=jnp.float32
    ).astype(jnp.bfloat16)
    full_query = jnp.concatenate([query_latent, selected[:, :, head_size:]], axis=2)
    scale = 1.0 / math.sqrt(full_query.shape[2] - latent_width + head_size)
    scores = (
        jnp.einsum("rhc,rtc->rht", full_query, latent_cache, preferred_element_type=jnp.float32)
        * scale
    )
    positions = jnp.arange(latent_cache.shape[1], dtype=jnp.int32)
    live = positions[None, None, :] < cache_lengths[:, None, None]
    scores = jnp.where(live, scores, -jnp.inf)
    highest = jnp.max(scores, axis=2, keepdims=True)
    weights = jnp.where(live, jnp.exp(scores - highest), 0.0)
    probs = (weights / jnp.sum(weights, axis=2, keepdims=True)).astype(jnp.bfloat16)
    context = jnp.einsum("rht,rtc->rhc", probs, latent_cache, preferred_element_type=jnp.float32)
    context = context[:, :, :latent_width].astype(jnp.bfloat16)
    heads_out = jnp.einsum(
        "rhc,hcd->rhd", context, absorb_value, preferred_element_type=jnp.float32
    ).astype(jnp.bfloat16)
    every_head = lax.all_gather(heads_out, "narrow", axis=1, tiled=True)
    flat_heads = every_head.reshape(slot_count, -1)
    head_columns = lax.all_to_all(flat_heads, "wide", split_axis=1, concat_axis=0, tiled=True)
    inverse = jnp.argsort(slot_rows)
    attention = lax.psum_scatter(
        jnp.dot(
            jnp.take(head_columns, inverse, axis=0), out_proj, preferred_element_type=jnp.float32
        ),
        "wide",
        scatter_dimension=0,
        tiled=True,
    )
    middle = residual_in.astype(jnp.float32) + attention
    square_sum = lax.psum(jnp.sum(middle * middle, axis=1), "narrow")
    normed = (
        middle * lax.rsqrt(square_sum / D + 1e-06)[:, None] * norm_gain.astype(jnp.float32)
    ).astype(jnp.bfloat16)
    hidden_cols = gate_weight.shape[1]
    row_piece = lax.all_gather(normed, "wide", axis=0, tiled=True)
    local_terms = jnp.concatenate(
        [
            jnp.dot(row_piece, gate_weight, preferred_element_type=jnp.float32),
            jnp.dot(row_piece, up_weight, preferred_element_type=jnp.float32),
        ],
        axis=1,
    )
    summed = lax.psum(local_terms, "narrow")
    hidden = (jax.nn.silu(summed[:, :hidden_cols]) * summed[:, hidden_cols:]).astype(jnp.bfloat16)
    ffn_total = lax.psum_scatter(
        jnp.dot(hidden, down_weight, preferred_element_type=jnp.float32),
        "wide",
        scatter_dimension=0,
        tiled=True,
    )
    return (middle + ffn_total).astype(jnp.bfloat16)


def solution(mesh):
    in_specs = (
        P("wide", "narrow"),
        P("wide", "narrow", None),
        P("wide", "narrow", None),
        P("narrow", None, None),
        P("narrow", None, None),
        P("wide", None, None),
        P("wide"),
        P(),
        P("wide", "narrow"),
        P("narrow"),
        P("narrow", "wide"),
        P("narrow", "wide"),
        P("wide", "narrow"),
    )
    out_specs = P("wide", "narrow")
    return jax.shard_map(shards, mesh=mesh, in_specs=in_specs, out_specs=out_specs, check_vma=False)
```

profile of v0, /device:TPU:2, one launch (start us, length us, event | category | flops | bytes accessed | tf_op | source)
XLA Modules:
  0.0 592.2 jit_solution(973563443931683544)
XLA Ops:
  6.5 0.0 copy-start
  6.5 0.9 compare_and_fusion
  7.4 0.7 pad_maximum_fusion.1
  8.2 53.8 %all_gather.9 = bf16[128,16,192]{2,1,0:T(8,128)(2,1)S(1)} all-gather(bf16[2,16,192]{2,1,0:T(8,128)(2,1)S(1)} %pad_maximum_fusion.1), channel_id=1, replica_groups=mesh['wide'=64,'narrow'=4] {'wide'}, dimensions={0}, use_global_device_ids=true | all-gather | bytes 798720 | tf_op jit(solution)/shard_map/all_gather | solution.py:30
  61.9 0.5 gather_fusion
  62.5 0.1 broadcast_select_fusion
  62.6 0.7 iota_compare_fusion
  63.3 0.0 copy-done
  63.3 0.4 fusion.21
  63.7 3.1 fusion.4
  66.8 0.2 fusion.29
  67.0 3.7 fusion.7
  70.8 0.0 copy-start.4
  70.8 0.0 copy-start.5
  70.8 0.0 copy-start.2
  70.8 0.0 copy-start.3
  70.8 2.0 fusion.5
  72.8 12.7 %all_gather.10 = bf16[2,64,128]{2,0,1:T(2,128)(2,1)} all-gather(bf16[2,16,128]{2,0,1:T(2,128)(2,1)S(1)} %fusion.5), channel_id=1, replica_groups=mesh['wide'=64,'narrow'=4] {'narrow'}, dimensions={1}, use_global_device_ids=true | all-gather | bytes 40960 | tf_op jit(solution)/shard_map/all_gather | solution.py:53
  85.6 6.7 %all-to-all-start = ((bf16[2,64,128]{2,0,1:T(2,128)(2,1)}), bf16[2,64,128]{2,0,1:T(2,128)(2,1)S(1)}, u32[]{:S(2)}, u32[]{:S(2)}) async-start(bf16[2,64,128]{2,0,1:T(2,128)(2,1)} %all_gather.10), calls=%async_computation | async-start | bytes 65536 | tf_op jit(solution)/shard_map/all_to_all | solution.py:55
  92.3 0.0 all-reduce.8.cloned.1.call-start
  92.4 0.0 copy-done.4
  92.4 2.5 sort.17
  94.9 6.9 %all-to-all-done = bf16[2,64,128]{2,0,1:T(2,128)(2,1)S(1)} async-done(((bf16[2,64,128]{2,0,1:T(2,128)(2,1)}), bf16[2,64,128]{2,0,1:T(2,128)(2,1)S(1)}, u32[]{:S(2)}, u32[]{:S(2)}) %all-to-all-start) | async-done | bytes 32800 | tf_op jit(solution)/shard_map/all_to_all | solution.py:55
  101.8 0.7 gather_fusion.1
  102.5 0.0 copy-done.1
  102.6 1.3 fusion.16
  103.9 0.0 all-reduce.8.cloned.1.call-update
  103.9 0.0 all-reduce.6.cloned.1.call-start
  103.9 0.0 copy-done.5
  103.9 0.6 dynamic-slice
  105.2 180.9 %all-reduce.8.cloned.1.call-done = f32[128,1792]{1,0:T(8,128)} async-done(((f32[128,1792]{1,0:T(8,128)}), f32[128,1792]{1,0:T(8,128)}) %all-reduce.8.cloned.1.call-update) | async-done | bytes 917520
  286.1 0.0 copy-done.2
  286.1 1.0 multiply_reduce_fusion
  287.0 0.0 copy-done.3
  287.0 8.6 %psum.14 = f32[2]{0:T(128)S(1)} all-reduce(f32[2]{0:T(128)S(1)} %multiply_reduce_fusion), channel_id=1, replica_groups=mesh['wide'=64,'narrow'=4] {'narrow'}, use_global_device_ids=true, to_apply=%region_5.6 | all-reduce | flops 2 | bytes 16 | tf_op jit(solution)/shard_map/psum | solution.py:66
  295.6 0.9 fusion.23
  296.5 48.1 %all-gather = bf16[64,2,1792]{2,1,0:T(2,128)(2,1)S(1)} all-gather(bf16[1,2,1792]{2,1,0:T(2,128)(2,1)S(1)} %fusion.23), channel_id=1, replica_groups=mesh['wide'=64,'narrow'=4] {'wide'}, dimensions={0}, use_global_device_ids=true | all-gather | bytes 465920 | tf_op jit(solution)/shard_map/all_gather | solution.py:71
  344.7 0.2 reshape.59
  344.8 1.6 fusion.31
  346.5 1.6 fusion.30
  348.1 0.7 pad_maximum_fusion
  348.9 0.0 all-reduce.6.cloned.1.call-update
  348.9 0.0 all-reduce.10.cloned.1.call-start
  349.0 42.7 %all-reduce.6.cloned.1.call-done = f32[128,576]{0,1:T(8,128)} async-done(((f32[128,576]{0,1:T(8,128)}), f32[128,576]{0,1:T(8,128)}) %all-reduce.6.cloned.1.call-update) | async-done | bytes 294928 | tf_op jit(solution)/shard_map/psum | solution.py:79
  391.7 2.8 fusion.9
  394.4 0.0 all-reduce.10.cloned.1.call-update
  394.5 189.7 %all-reduce.10.cloned.1.call-done = f32[128,1792]{1,0:T(8,128)} async-done(((f32[128,1792]{1,0:T(8,128)}), f32[128,1792]{1,0:T(8,128)}) %all-reduce.10.cloned.1.call-update) | async-done | bytes 917520
  584.2 1.5 fusion.20
  (12 shorter events, 0.1 us)
Async XLA Ops:
  6.5 56.8 %copy-start = (bf16[16,128,512]{2,1,0:T(8,128)(2,1)S(1)}, bf16[16,128,512]{2,1,0:T(8,128)(2,1)}, u32[]{:S(2)}) copy-start(bf16[16,128,512]{2,1,0:T(8,128)(2,1)} %param.16) | copy-start | bytes 6291460
  70.8 21.6 %copy-start.4 = (s32[128]{0:T(128)S(1)}, s32[128]{0:T(128)}, u32[]{:S(2)}) copy-start(s32[128]{0:T(128)} %param.20) | copy-start | bytes 1540
  70.8 31.8 %copy-start.1 = (bf16[128,1792]{1,0:T(8,128)(2,1)S(1)}, bf16[128,1792]{1,0:T(8,128)(2,1)}, u32[]{:S(2)}) copy-start(bf16[128,1792]{1,0:T(8,128)(2,1)} %param.21) | copy-start | bytes 1376260
  70.8 33.2 %copy-start.5 = (u32[256]{0:T(256)S(1)}, u32[256]{0:T(256)}, u32[]{:S(2)}) copy-start(u32[256]{0:T(256)} %constant.62) | copy-start | bytes 3076
  70.8 215.3 %copy-start.2 = (bf16[2,1792]{1,0:T(2,128)(2,1)S(1)}, bf16[2,1792]{1,0:T(2,128)(2,1)}, u32[]{:S(2)}) copy-start(bf16[2,1792]{1,0:T(2,128)(2,1)} %param.13) | copy-start | bytes 21508
  70.8 216.2 %copy-start.3 = (bf16[1792]{0:T(1024)(128)(2,1)S(1)}, bf16[1792]{0:T(1024)(128)(2,1)}, u32[]{:S(2)}) copy-start(bf16[1792]{0:T(1024)(128)(2,1)} %param.22) | copy-start | bytes 10756
  85.6 16.3 %all-to-all-start = ((bf16[2,64,128]{2,0,1:T(2,128)(2,1)}), bf16[2,64,128]{2,0,1:T(2,128)(2,1)S(1)}, u32[]{:S(2)}, u32[]{:S(2)}) async-start(bf16[2,64,128]{2,0,1:T(2,128)(2,1)} %all_gather.10), calls=%async_computation | async-start | bytes 65536 | tf_op jit(solution)/shard_map/all_to_all | solution.py:55
  92.3 193.7 %all-reduce.8.cloned.1.call-start = ((), (), s32[]{:S(2)}) async-start(), calls=%async_computation.2 | async-start | bytes 1835008
  103.9 287.8 %all-reduce.6.cloned.1.call-start = ((), (), s32[]{:S(2)}) async-start(), calls=%async_computation.1 | async-start | bytes 589824 | tf_op jit(solution)/shard_map/psum | solution.py:79
  348.9 235.3 %all-reduce.10.cloned.1.call-start = ((), (), s32[]{:S(2)}) async-start(), calls=%async_computation.3 | async-start | bytes 1835008
Sparse Core Ops, SparseCore 0:
  104.0 182.0 all-reduce.7
  349.0 42.5 all-reduce.5
  395.1 189.0 all-reduce.9
where the time goes:
time: 593 us; the launch traced here: 592 us
  waiting for transfers between devices  420 us (71%)
  blocking collectives  123 us (21%)
  matrix products  16.6 us (3%)
  between operations  13.9 us (2%)
  other arithmetic  9.27 us (2%)
  starting transfers between devices  6.87 us (1%)
    unnamed x5, waiting for transfers between devices  371 us
    all_gather x1, blocking collectives, shards(): gathered = lax.all_gather(packed_queries, 'wide', axis=0, tiled=True)  53.8 us
    all_gather x1, blocking collectives, shards(): row_piece = lax.all_gather(normed, 'wide', axis=0, tiled=True)  48.1 us
    psum x1, waiting for transfers between devices, shards(): summed = lax.psum(local_terms, 'narrow')  42.7 us
    all_gather x1, blocking collectives, shards(): every_head = lax.all_gather(heads_out, 'narrow', axis=1, tiled=True)  12.7 us
  transfers between devices with their start and end apart: 4, of which 4 were waited for; matrix products, arithmetic and copies ran while one was open for 1% of the time, Pallas kernels for 0%

commit v1 on v0

--- a/solution.py
+++ b/solution.py
@@ -68,7 +68,9 @@
         middle * lax.rsqrt(square_sum / D + 1e-06)[:, None] * norm_gain.astype(jnp.float32)
     ).astype(jnp.bfloat16)
     hidden_cols = gate_weight.shape[1]
-    row_piece = lax.all_gather(normed, "wide", axis=0, tiled=True)
+    row_piece = jnp.concatenate(
+        lax.all_to_all(jnp.stack([normed] * lax.axis_size("wide")), "wide", 0, 0), axis=0
+    )
     local_terms = jnp.concatenate(
         [
             jnp.dot(row_piece, gate_weight, preferred_element_type=jnp.float32),

time: 593 us -> 567 us (0.956)
  blocking collectives: 123 us -> 96.9 us
    all_gather x1 -> x0, blocking collectives: 48.1 us -> none  [shards(): row_piece = lax.all_gather(normed, 'wide', axis=0, tiled=True)]
    all_to_all x0 -> x1, blocking collectives: none -> 21.8 us  [shards(): lax.all_to_all(jnp.stack([normed] * lax.axis_size('wide')), 'wide', 0, 0)]
where the time goes in v1:
time: 567 us; the launch traced here: 566 us
  waiting for transfers between devices  421 us (74%)
  blocking collectives  96.9 us (17%)
  matrix products  16.6 us (3%)
  between operations  13.9 us (2%)
  other arithmetic  9.27 us (2%)
  starting transfers between devices  6.87 us (1%)
    unnamed x5, waiting for transfers between devices  371 us
    all_gather x1, blocking collectives, shards(): gathered = lax.all_gather(packed_queries, 'wide', axis=0, tiled=True)  53.8 us
    psum x1, waiting for transfers between devices, shards(): summed = lax.psum(local_terms, 'narrow')  43 us
    all_to_all x1, blocking collectives, shards(): lax.all_to_all(jnp.stack([normed] * lax.axis_size('wide')), 'wide', 0, 0)  21.8 us
    all_gather x1, blocking collectives, shards(): every_head = lax.all_gather(heads_out, 'narrow', axis=1, tiled=True)  12.7 us
  transfers between devices with their start and end apart: 4, of which 4 were waited for; matrix products, arithmetic and copies ran while one was open for 1% of the time, Pallas kernels for 0%

profile of v1, /device:TPU:2, one launch (start us, length us, event | category | flops | bytes accessed | tf_op | source)
XLA Modules:
  0.0 566.4 jit_solution(4672036325003185839)
XLA Ops:
  6.5 0.0 copy-start
  6.5 0.9 compare_and_fusion
  7.4 0.7 pad_maximum_fusion.1
  8.2 53.8 %all_gather.6 = bf16[128,16,192]{2,1,0:T(8,128)(2,1)S(1)} all-gather(bf16[2,16,192]{2,1,0:T(8,128)(2,1)S(1)} %pad_maximum_fusion.1), channel_id=1, replica_groups=mesh['wide'=64,'narrow'=4] {'wide'}, dimensions={0}, use_global_device_ids=true | all-gather | bytes 798720 | tf_op jit(solution)/shard_map/all_gather | solution.py:30
  61.9 0.5 gather_fusion
  62.5 0.1 broadcast_select_fusion
  62.6 0.7 iota_compare_fusion
  63.3 0.0 copy-done
  63.3 0.4 fusion.21
  63.7 3.1 fusion.4
  66.8 0.2 fusion.28
  67.0 3.7 fusion.7
  70.8 0.0 copy-start.5
  70.8 0.0 copy-start.2
  70.8 0.0 copy-start.3
  70.8 2.0 fusion.5
  72.8 12.7 %all_gather.7 = bf16[2,64,128]{2,0,1:T(2,128)(2,1)} all-gather(bf16[2,16,128]{2,0,1:T(2,128)(2,1)S(1)} %fusion.5), channel_id=1, replica_groups=mesh['wide'=64,'narrow'=4] {'narrow'}, dimensions={1}, use_global_device_ids=true | all-gather | bytes 40960 | tf_op jit(solution)/shard_map/all_gather | solution.py:53
  85.6 6.7 %all-to-all-start = ((bf16[2,64,128]{2,0,1:T(2,128)(2,1)}), bf16[2,64,128]{2,0,1:T(2,128)(2,1)S(1)}, u32[]{:S(2)}, u32[]{:S(2)}) async-start(bf16[2,64,128]{2,0,1:T(2,128)(2,1)} %all_gather.7), calls=%async_computation | async-start | bytes 65536 | tf_op jit(solution)/shard_map/all_to_all | solution.py:55
  92.3 0.0 all-reduce.8.cloned.1.call-start
  92.4 0.0 copy-done.4
  92.4 2.5 sort.17
  94.9 6.9 %all-to-all-done = bf16[2,64,128]{2,0,1:T(2,128)(2,1)S(1)} async-done(((bf16[2,64,128]{2,0,1:T(2,128)(2,1)}), bf16[2,64,128]{2,0,1:T(2,128)(2,1)S(1)}, u32[]{:S(2)}, u32[]{:S(2)}) %all-to-all-start) | async-done | bytes 32800 | tf_op jit(solution)/shard_map/all_to_all | solution.py:55
  101.8 0.7 gather_fusion.1
  102.5 0.0 copy-done.1
  102.6 1.3 fusion.16
  103.9 0.0 all-reduce.8.cloned.1.call-update
  103.9 0.0 all-reduce.6.cloned.1.call-start
  103.9 0.0 copy-done.5
  103.9 0.6 dynamic-slice
  105.2 180.9 %all-reduce.8.cloned.1.call-done = f32[128,1792]{1,0:T(8,128)} async-done(((f32[128,1792]{1,0:T(8,128)}), f32[128,1792]{1,0:T(8,128)}) %all-reduce.8.cloned.1.call-update) | async-done | bytes 917520
  286.1 0.0 copy-done.2
  286.1 1.0 multiply_reduce_fusion
  287.0 0.0 copy-done.3
  287.0 8.6 %psum.14 = f32[2]{0:T(128)S(1)} all-reduce(f32[2]{0:T(128)S(1)} %multiply_reduce_fusion), channel_id=1, replica_groups=mesh['wide'=64,'narrow'=4] {'narrow'}, use_global_device_ids=true, to_apply=%region_5.6 | all-reduce | flops 2 | bytes 16 | tf_op jit(solution)/shard_map/psum | solution.py:66
  295.6 0.9 multiply_convert_fusion
  296.5 0.2 stack.2
  296.8 21.8 %all_to_all.21 = bf16[64,2,1792]{2,1,0:T(2,128)(2,1)S(1)} all-to-all(bf16[64,2,1792]{2,1,0:T(2,128)(2,1)S(1)} %stack.2), channel_id=1, replica_groups=mesh['wide'=64,'narrow'=4] {'wide'}, dimensions={0} | all-to-all | bytes 917504 | tf_op jit(solution)/shard_map/all_to_all | solution.py:72
  318.6 0.2 reshape.45
  318.7 1.6 fusion.30
  320.4 1.6 fusion.29
  322.0 0.7 pad_maximum_fusion
  322.8 0.0 all-reduce.6.cloned.1.call-update
  322.8 0.0 all-reduce.10.cloned.1.call-start
  322.9 43.0 %all-reduce.6.cloned.1.call-done = f32[128,576]{0,1:T(8,128)} async-done(((f32[128,576]{0,1:T(8,128)}), f32[128,576]{0,1:T(8,128)}) %all-reduce.6.cloned.1.call-update) | async-done | bytes 294928 | tf_op jit(solution)/shard_map/psum | solution.py:81
  365.9 2.8 fusion.9
  368.6 0.0 all-reduce.10.cloned.1.call-update
  368.7 189.7 %all-reduce.10.cloned.1.call-done = f32[128,1792]{1,0:T(8,128)} async-done(((f32[128,1792]{1,0:T(8,128)}), f32[128,1792]{1,0:T(8,128)}) %all-reduce.10.cloned.1.call-update) | async-done | bytes 917520
  558.4 1.5 fusion.20
  (13 shorter events, 0.1 us)
Async XLA Ops:
  6.5 56.8 %copy-start = (bf16[16,128,512]{2,1,0:T(8,128)(2,1)S(1)}, bf16[16,128,512]{2,1,0:T(8,128)(2,1)}, u32[]{:S(2)}) copy-start(bf16[16,128,512]{2,1,0:T(8,128)(2,1)} %param.16) | copy-start | bytes 6291460
  70.8 21.6 %copy-start.4 = (s32[128]{0:T(128)S(1)}, s32[128]{0:T(128)}, u32[]{:S(2)}) copy-start(s32[128]{0:T(128)} %param.20) | copy-start | bytes 1540
  70.8 31.8 %copy-start.1 = (bf16[128,1792]{1,0:T(8,128)(2,1)S(1)}, bf16[128,1792]{1,0:T(8,128)(2,1)}, u32[]{:S(2)}) copy-start(bf16[128,1792]{1,0:T(8,128)(2,1)} %param.21) | copy-start | bytes 1376260
  70.8 33.2 %copy-start.5 = (u32[256]{0:T(256)S(1)}, u32[256]{0:T(256)}, u32[]{:S(2)}) copy-start(u32[256]{0:T(256)} %constant.62) | copy-start | bytes 3076
  70.8 215.3 %copy-start.2 = (bf16[2,1792]{1,0:T(2,128)(2,1)S(1)}, bf16[2,1792]{1,0:T(2,128)(2,1)}, u32[]{:S(2)}) copy-start(bf16[2,1792]{1,0:T(2,128)(2,1)} %param.13) | copy-start | bytes 21508
  70.8 216.2 %copy-start.3 = (bf16[1792]{0:T(1024)(128)(2,1)S(1)}, bf16[1792]{0:T(1024)(128)(2,1)}, u32[]{:S(2)}) copy-start(bf16[1792]{0:T(1024)(128)(2,1)} %param.22) | copy-start | bytes 10756
  85.6 16.3 %all-to-all-start = ((bf16[2,64,128]{2,0,1:T(2,128)(2,1)}), bf16[2,64,128]{2,0,1:T(2,128)(2,1)S(1)}, u32[]{:S(2)}, u32[]{:S(2)}) async-start(bf16[2,64,128]{2,0,1:T(2,128)(2,1)} %all_gather.7), calls=%async_computation | async-start | bytes 65536 | tf_op jit(solution)/shard_map/all_to_all | solution.py:55
  92.3 193.7 %all-reduce.8.cloned.1.call-start = ((), (), s32[]{:S(2)}) async-start(), calls=%async_computation.3 | async-start | bytes 1835008
  103.9 262.0 %all-reduce.6.cloned.1.call-start = ((), (), s32[]{:S(2)}) async-start(), calls=%async_computation.2 | async-start | bytes 589824 | tf_op jit(solution)/shard_map/psum | solution.py:81
  322.8 235.6 %all-reduce.10.cloned.1.call-start = ((), (), s32[]{:S(2)}) async-start(), calls=%async_computation.4 | async-start | bytes 1835008
Sparse Core Ops, SparseCore 0:
  104.0 182.0 all-reduce.7
  322.9 42.8 all-reduce.5
  369.3 189.0 all-reduce.9
